TPU v7x, 32 devices: a whole 2x2x4 slice. The times are simulated.
32 devices in a mesh: seq: 4 (over z), expert: 8 (over y, x, core).
Axes of the slice: x: 2, y: 2, z: 4, core: 2. Of those that a mesh axis runs over, the one named last changes fastest.
Arguments:
- residual: bfloat16 [8, 512, 2048], P('expert', 'seq'), may hold values from -6 to 6
- queries: bfloat16 [8, 512, 2048], P('expert', 'seq'), may hold values from -400 to 400
- key_input: bfloat16 [8, 512, 512], P('expert', 'seq'), may hold values from -4 to 4
- value_input: bfloat16 [8, 512, 512], P('expert', 'seq'), may hold values from -6 to 6
- routes: int32 [8, 512, 6], P('expert', 'seq'), may hold values from 0 to 15, all different within a row; in each aligned block of 128 rows (0 to 127, 128 to 255, ..., all dimensions but the last counted through in order) at most 60 rows name the same one
- mix_weights: float32 [8, 512, 6], P('expert', 'seq'), may hold values from 0.1 to 1
- gate_weight: bfloat16 [16, 2048, 704], P('expert'), may hold values from -0.125 to 0.125
- up_weight: bfloat16 [16, 2048, 704], P('expert'), may hold values from -0.125 to 0.125
- down_weight: bfloat16 [16, 704, 2048], P('expert'), may hold values from -0.21875 to 0.21875
- grad_out: bfloat16 [8, 512, 2048], P('expert', 'seq'), may hold values from -6 to 6
Outputs:
- layer_out: bfloat16 [8, 512, 2048], P('expert', 'seq')
- residual_grad: bfloat16 [8, 512, 2048], P('expert', 'seq')
- query_grad: bfloat16 [8, 512, 2048], P('expert', 'seq')
- key_grad: bfloat16 [8, 512, 512], P('expert', 'seq')
- value_grad: bfloat16 [8, 512, 512], P('expert', 'seq')
- mix_grad: float32 [8, 512, 6], P('expert', 'seq')
- gate_weight_grad: bfloat16 [16, 2048, 704], P('expert', 'seq')
- up_weight_grad: bfloat16 [16, 2048, 704], P('expert', 'seq')
- down_weight_grad: bfloat16 [16, 704, 2048], P('expert', None, 'seq')
Inputs may be any that keep to these rules, and one draw needn't show every extreme that they name: `routes`: each row names 6 different experts. Among the rows of one device no expert is named by more than 60 rows, and in every draw some expert is named by exactly 60 rows of some device.
All inputs are finite; a program needn't handle non-finite values.
Results may differ from a plain program's by a relative error of at most 0.04.
Values may be sent and summed in bfloat16 or wider, within the bound.
A program may use at most 192 MiB of HBM per device.

v0:
```python
import functools
import math

import jax
import jax.numpy as jnp
from jax import lax
from jax.experimental import pallas as pl
from jax.experimental.pallas import tpu as pltpu
from jax.sharding import PartitionSpec as P

DH = 128
neg_big = -1e30
norm_eps = 1e-06
BF = jnp.bfloat16
F32 = jnp.float32
GATHER_BYTES = 32 * 1024 * 1024
VMEM_LIMIT = 56 * 1024 * 1024


def dot(a, b, ca, cb):
    return lax.dot_general(a, b, (((ca,), (cb,)), ((), ())), preferred_element_type=F32)


def vm():
    return pl.BlockSpec(memory_space=pltpu.VMEM)


def heads_of(ref, first, count):
    return jnp.concatenate(
        [ref[:, (first + g) * DH : (first + g + 1) * DH] for g in range(count)], axis=0
    )


def visible_mask(tokens, group, full, seq_index):
    shape = (group, tokens, full)
    pos = lax.broadcasted_iota(jnp.int32, shape, 1) + seq_index * tokens
    key = lax.broadcasted_iota(jnp.int32, shape, 2)
    return (key <= pos).reshape(group * tokens, full)


def attend_kernel(group, residual, q, kv, att, log_total, inv_rms, normed):
    tokens = q.shape[0]
    full = kv.shape[0]
    kv_heads = kv.shape[1] // (2 * DH)
    visible = visible_mask(tokens, group, full, lax.axis_index("seq"))
    scale = 1.0 / math.sqrt(DH)
    for k in range(kv_heads):
        qh = heads_of(q, k * group, group)
        kh = kv[:, k * DH : (k + 1) * DH]
        vh = kv[:, (kv_heads + k) * DH : (kv_heads + k + 1) * DH]
        scores = jnp.where(visible, dot(qh, kh, 1, 1) * scale, neg_big)
        top = jnp.max(scores, axis=1, keepdims=True)
        weights = jnp.exp(scores - top)
        total = jnp.sum(weights, axis=1, keepdims=True)
        out = (dot(weights.astype(BF), vh, 1, 0) / total).astype(BF)
        logs = top + jnp.log(total)
        for g in range(group):
            h = k * group + g
            att[:, h * DH : (h + 1) * DH] = out[g * tokens : (g + 1) * tokens]
            log_total[:, h : h + 1] = logs[g * tokens : (g + 1) * tokens]
    hidden = residual[...].astype(F32) + att[...].astype(F32)
    inv = lax.rsqrt(jnp.mean(hidden * hidden, axis=1, keepdims=True) + norm_eps)
    inv_rms[...] = inv
    normed[...] = (hidden * inv).astype(BF)


def attend(residual, q, kv, group):
    tokens, width = q.shape
    heads = width // DH
    return pl.pallas_call(
        functools.partial(attend_kernel, group),
        out_shape=(
            jax.ShapeDtypeStruct((tokens, width), BF),
            jax.ShapeDtypeStruct((tokens, heads), F32),
            jax.ShapeDtypeStruct((tokens, 1), F32),
            jax.ShapeDtypeStruct((tokens, width), BF),
        ),
        in_specs=[vm()] * 3,
        out_specs=(vm(),) * 4,
        compiler_params=pltpu.CompilerParams(vmem_limit_bytes=VMEM_LIMIT),
        cost_estimate=pl.CostEstimate(
            flops=4 * tokens * kv.shape[0] * width,
            bytes_accessed=8 * tokens * width + 2 * kv.size,
            transcendentals=heads * tokens * kv.shape[0],
        ),
        name="attend",
    )(residual, q, kv)


def attend_back_kernel(
    group, residual, q, kv, att, log_total, inv_rms, grad_out, normed_grad, res_grad, q_grad, kv_part
):
    tokens = q.shape[0]
    full = kv.shape[0]
    kv_heads = kv.shape[1] // (2 * DH)
    scale = 1.0 / math.sqrt(DH)
    inv = inv_rms[...]
    normed = (residual[...].astype(F32) + att[...].astype(F32)) * inv
    ngrad = normed_grad[...].astype(F32)
    dot_mean = jnp.mean(ngrad * normed, axis=1, keepdims=True)
    res_grad[...] = (grad_out[...].astype(F32) + inv * (ngrad - normed * dot_mean)).astype(BF)
    visible = visible_mask(tokens, group, full, lax.axis_index("seq"))
    for k in range(kv_heads):
        qh = heads_of(q, k * group, group)
        oh = heads_of(att, k * group, group)
        gh = heads_of(res_grad, k * group, group)
        logs = jnp.concatenate(
            [log_total[:, k * group + g : k * group + g + 1] for g in range(group)], axis=0
        )
        kh = kv[:, k * DH : (k + 1) * DH]
        vh = kv[:, (kv_heads + k) * DH : (kv_heads + k + 1) * DH]
        scores = jnp.where(visible, dot(qh, kh, 1, 1) * scale, neg_big)
        probs = jnp.exp(scores - logs)
        delta = jnp.sum(gh.astype(F32) * oh.astype(F32), axis=1, keepdims=True)
        pgrad = dot(gh, vh, 1, 1)
        sgrad = (probs * (pgrad - delta)).astype(BF)
        dq = (dot(sgrad, kh, 1, 0) * scale).astype(BF)
        for g in range(group):
            h = k * group + g
            q_grad[:, h * DH : (h + 1) * DH] = dq[g * tokens : (g + 1) * tokens]
        kv_part[:, k * DH : (k + 1) * DH] = (dot(sgrad, qh, 0, 0) * scale).astype(BF)
        kv_part[:, (kv_heads + k) * DH : (kv_heads + k + 1) * DH] = dot(
            probs.astype(BF), gh, 0, 0
        ).astype(BF)


def attend_back(group, residual, q, kv, att, log_total, inv_rms, grad_out, normed_grad):
    tokens, width = q.shape
    return pl.pallas_call(
        functools.partial(attend_back_kernel, group),
        out_shape=(
            jax.ShapeDtypeStruct((tokens, width), BF),
            jax.ShapeDtypeStruct((tokens, width), BF),
            jax.ShapeDtypeStruct(kv.shape, BF),
        ),
        in_specs=[vm()] * 8,
        out_specs=(vm(),) * 3,
        compiler_params=pltpu.CompilerParams(vmem_limit_bytes=VMEM_LIMIT),
        cost_estimate=pl.CostEstimate(
            flops=10 * tokens * kv.shape[0] * width,
            bytes_accessed=14 * tokens * width + 4 * kv.size,
            transcendentals=tokens * kv.shape[0] * (width // DH),
        ),
        name="attend_back",
    )(residual, q, kv, att, log_total, inv_rms, grad_out, normed_grad)


def pick_kernel(seq_index, slot, rows, picked):
    local = slot.shape[2]
    depth = picked.shape[1]
    tokens = rows.shape[2]
    row = lax.broadcasted_iota(jnp.int32, (depth, tokens), 0)
    for e in range(local):
        chosen = (slot[0, 0, e : e + 1, :] == row).astype(F32).astype(BF)
        picked[e] = dot(chosen, rows[0, 0], 1, 0).astype(BF)


def pick_rows(gathered, slot, seq_index, first, planes, depth):
    seqs, ranks, tokens, width = gathered.shape
    local = slot.shape[2]
    count = planes * ranks

    def source(i, s):
        return (lax.rem(s[0] + first + i // ranks, seqs), lax.rem(i, ranks), 0, 0)

    return pl.pallas_call(
        pick_kernel,
        out_shape=jax.ShapeDtypeStruct((local, count * depth, width), BF),
        grid_spec=pltpu.PrefetchScalarGridSpec(
            num_scalar_prefetch=1,
            grid=(count,),
            in_specs=[
                pl.BlockSpec((1, 1, local, tokens), source),
                pl.BlockSpec((1, 1, tokens, width), source),
            ],
            out_specs=pl.BlockSpec((local, depth, width), lambda i, s: (0, i, 0)),
        ),
        compiler_params=pltpu.CompilerParams(vmem_limit_bytes=16 * 1024 * 1024),
        cost_estimate=pl.CostEstimate(
            flops=2 * local * count * depth * tokens * width,
            bytes_accessed=2 * count * (tokens + local * depth) * width,
            transcendentals=0,
        ),
        name="pick_rows",
    )(seq_index, slot, gathered)


def spread_kernel(slot, rows, out):
    ranks, local, tokens = slot.shape
    depth = rows.shape[1]
    row = lax.broadcasted_iota(jnp.int32, (depth, tokens), 0)
    total = None
    for e in range(local):
        chosen = (slot[0, e : e + 1, :] == row).astype(F32).astype(BF)
        part = dot(chosen, rows[e], 0, 0)
        total = part if total is None else total + part
    out[0] = total.astype(BF)


def spread_rows(rows, slot):
    ranks, local, tokens = slot.shape
    width = rows.shape[2]
    depth = rows.shape[1] // ranks
    return pl.pallas_call(
        spread_kernel,
        out_shape=jax.ShapeDtypeStruct((ranks, tokens, width), BF),
        grid=(ranks,),
        in_specs=[
            pl.BlockSpec((1, local, tokens), lambda i: (i, 0, 0)),
            pl.BlockSpec((local, depth, width), lambda i: (0, i, 0)),
        ],
        out_specs=pl.BlockSpec((1, tokens, width), lambda i: (i, 0, 0)),
        compiler_params=pltpu.CompilerParams(vmem_limit_bytes=16 * 1024 * 1024),
        cost_estimate=pl.CostEstimate(
            flops=2 * local * ranks * depth * tokens * width,
            bytes_accessed=2 * ranks * (tokens + local * depth) * width,
            transcendentals=0,
        ),
        name="spread_rows",
    )(slot, rows)


def hidden_units(rows, grads, mix, gate_weight, up_weight, down_weight):
    gate_pre = jnp.einsum("erd,edf->erf", rows, gate_weight, preferred_element_type=F32)
    up_pre = jnp.einsum("erd,edf->erf", rows, up_weight, preferred_element_type=F32)
    raw = jnp.einsum("erd,efd->erf", grads, down_weight, preferred_element_type=F32)
    sigmoid = jax.nn.sigmoid(gate_pre)
    silu = gate_pre * sigmoid
    act = silu * up_pre
    act_grad = raw * mix[:, :, None]
    gate_grad = (act_grad * up_pre * sigmoid * (1.0 + gate_pre * (1.0 - sigmoid))).astype(BF)
    up_grad = (act_grad * silu).astype(BF)
    mixed = (act * mix[:, :, None]).astype(BF)
    return (gate_grad, up_grad, mixed, act, raw)


def on_device(
    residual,
    queries,
    key_input,
    value_input,
    routes,
    mix_weights,
    gate_weight,
    up_weight,
    down_weight,
    grad_out,
):
    tokens = residual.shape[1]
    width = residual.shape[2]
    kv_width = key_input.shape[2]
    group = queries.shape[2] // kv_width
    local = gate_weight.shape[0]
    ranks = lax.axis_size("expert")
    seqs = lax.axis_size("seq")
    experts = local * ranks
    top_count = routes.shape[2]
    capacity = tokens * top_count * 5 // (4 * experts)
    depth = -(-capacity // 16) * 16
    both = ("seq", "expert")
    seq_index = lax.axis_index("seq")
    rank_index = lax.axis_index("expert")
    seq_array = seq_index.astype(jnp.int32).reshape(1)

    kv_mine = jnp.concatenate(
        [key_input.reshape(tokens, kv_width), value_input.reshape(tokens, kv_width)], axis=1
    )
    kv = lax.all_gather(kv_mine, "seq", axis=0, tiled=True)

    expert_ids = jnp.arange(experts, dtype=jnp.int32)
    picked = routes.reshape(tokens, top_count)
    mix_rows = mix_weights.reshape(tokens, top_count)
    hit = picked[None, :, :] == expert_ids[:, None, None]
    table = jnp.sum(jnp.where(hit, mix_rows[None], 0.0), axis=2) - (
        1.0 - jnp.sum(hit.astype(F32), axis=2)
    )
    tables = lax.all_gather(table, both, axis=0, tiled=False)
    mine = lax.dynamic_slice_in_dim(tables, rank_index * local, local, axis=1)
    routed = mine >= 0.0
    before = jnp.triu(jnp.ones((tokens, tokens), BF), 1)
    rank = jnp.einsum("bet,tu->beu", routed.astype(BF), before, preferred_element_type=F32)
    slot = jnp.where(routed, rank.astype(jnp.int32), -1)
    slot = slot.reshape(seqs, ranks, local, tokens)
    mine = mine.reshape(seqs, ranks, local, tokens)

    grad_rows = grad_out.reshape(tokens, width)
    grads_all = lax.all_gather(grad_rows, both, axis=0, tiled=True)
    grads_all = grads_all.reshape(seqs, ranks, tokens, width)

    q = queries.reshape(tokens, width)
    res = residual.reshape(tokens, width)
    att, log_total, inv_rms, normed_bf = attend(res, q, kv, group)
    grads_own = pick_rows(grads_all, slot, seq_array, 0, 1, depth)
    grads_far = pick_rows(grads_all, slot, seq_array, 1, seqs - 1, depth)
    if 2 * grads_all.size > GATHER_BYTES:
        normed_bf, grads_own, grads_far = lax.optimization_barrier(
            (normed_bf, grads_own, grads_far)
        )
    normed_all = lax.all_gather(normed_bf, both, axis=0, tiled=True)
    normed_all = normed_all.reshape(seqs, ranks, tokens, width)

    slot_turned = jnp.roll(slot, -seq_index, axis=0)
    mix_turned = jnp.roll(mine, -seq_index, axis=0)
    here = slot_turned[..., None, :] == jnp.arange(depth, dtype=jnp.int32)[:, None]
    mix_slot = jnp.sum(jnp.where(here, mix_turned[..., None, :], 0.0), axis=4)
    mix_slot = jnp.transpose(mix_slot, (2, 0, 1, 3)).reshape(local, seqs * ranks * depth)
    own = ranks * depth

    rows_own = pick_rows(normed_all, slot, seq_array, 0, 1, depth)
    rows_far = pick_rows(normed_all, slot, seq_array, 1, seqs - 1, depth)
    weights = (gate_weight, up_weight, down_weight)
    gate_own, up_own, mixed_own, act_own, raw_own = hidden_units(
        rows_own, grads_own, mix_slot[:, :own], *weights
    )
    input_grad = (
        jnp.einsum("erf,edf->erd", gate_own, gate_weight, preferred_element_type=F32)
        + jnp.einsum("erf,edf->erd", up_own, up_weight, preferred_element_type=F32)
    ).astype(BF)
    slot_own = slot_turned[0]
    input_part = spread_rows(input_grad, slot_own).reshape(ranks * tokens, width)
    normed_grad = lax.psum_scatter(input_part, "expert", scatter_dimension=0, tiled=True)

    expert_out = jnp.einsum(
        "erf,efd->erd", mixed_own, down_weight, preferred_element_type=F32
    ).astype(BF)
    out_part = spread_rows(expert_out, slot_own).reshape(ranks * tokens, width)
    routed_out = lax.psum_scatter(out_part, "expert", scatter_dimension=0, tiled=True)
    hidden = res.astype(F32) + att.astype(F32)
    layer_out = (hidden + routed_out.astype(F32)).astype(BF)

    pair_dot = jnp.sum(act_own.astype(BF).astype(F32) * raw_own, axis=2)
    pair_dot = pair_dot.reshape(local, ranks, depth)
    token_dot = jnp.sum(
        jnp.where(here[0], jnp.transpose(pair_dot, (1, 0, 2))[..., None], 0.0), axis=2
    )
    dots = lax.all_to_all(token_dot, "expert", split_axis=0, concat_axis=0, tiled=True)
    dots = dots.reshape(experts, tokens)
    mix_grad = jnp.sum(jnp.where(hit, dots[:, :, None], 0.0), axis=0)

    gate_far, up_far, mixed_far, _, _ = hidden_units(
        rows_far, grads_far, mix_slot[:, own:], *weights
    )
    share = width // seqs

    def columns(array):
        return lax.dynamic_slice_in_dim(array, seq_index * share, share, axis=2)

    def outer(a_own, a_far, b_own, b_far):
        return (
            jnp.einsum("erm,ern->emn", a_own, b_own, preferred_element_type=F32)
            + jnp.einsum("erm,ern->emn", a_far, b_far, preferred_element_type=F32)
        ).astype(BF)

    cols_own, cols_far = columns(rows_own), columns(rows_far)
    gate_share = outer(cols_own, cols_far, gate_own, gate_far)
    up_share = outer(cols_own, cols_far, up_own, up_far)
    down_share = outer(mixed_own, mixed_far, columns(grads_own), columns(grads_far))

    res_grad, q_grad, kv_part = attend_back(
        group, res, q, kv, att, log_total, inv_rms, grad_rows, normed_grad
    )
    kv_share = lax.psum_scatter(kv_part, "seq", scatter_dimension=0, tiled=True)
    return (
        layer_out.reshape(1, tokens, width),
        res_grad.reshape(1, tokens, width),
        q_grad.reshape(1, tokens, width),
        kv_share[:, :kv_width].reshape(1, tokens, kv_width),
        kv_share[:, kv_width:].reshape(1, tokens, kv_width),
        mix_grad.reshape(1, tokens, top_count),
        gate_share,
        up_share,
        down_share,
    )


def solution(mesh):
    rows = P("expert", "seq", None)
    weight = P("expert", None, None)
    return jax.shard_map(
        on_device,
        mesh=mesh,
        in_specs=(rows,) * 6 + (weight,) * 3 + (rows,),
        out_specs=(rows,) * 8 + (P("expert", None, "seq"),),
        check_vma=False,
    )
```

profile of v0, /device:TPU:19, one launch (start us, length us, event | category | flops | bytes accessed | tf_op | source)
XLA Modules:
  0.0 466.7 jit_solution(11704962719455921130)
XLA Ops:
  9.7 28.4 %all-gather.6.cloned.1.call-done.kv = bf16[512,1024]{1,0:T(8,128)(2,1)} async-done(((bf16[128,1024]{1,0:T(8,128)(2,1)}), bf16[512,1024]{1,0:T(8,128)(2,1)}) %all-gather.6.cloned.1.call-update) | async-done | bytes 1048592 | tf_op jit(solution)/shard_map/all_gather | solution.py:268
  38.1 4.6 attend.1
  44.2 32.6 %all-gather = f32[512,128]{1,0:T(8,128)S(1)} all-gather(f32[16,128]{1,0:T(8,128)S(1)} %subtract_subtract_fusion), channel_id=2, replica_groups=mesh['seq'=4,'expert'=8] {'seq','expert'}, dimensions={0}, use_global_device_ids=true | all-gather | bytes 270336 | tf_op jit(solution)/shard_map/all_gather | solution.py:277
  79.5 76.6 %all-gather.10.cloned.1.call-done = bf16[1,4096,2048]{2,1,0:T(8,128)(2,1)} async-done(((bf16[1,128,2048]{2,1,0:T(8,128)(2,1)}), bf16[1,4096,2048]{2,1,0:T(8,128)(2,1)}) %all-gather.10.cloned.1.call-update) | async-done | bytes 16777232 | tf_op jit(solution)/shard_map/all_gather | solution.py:287
  156.1 5.8 %copy-done.1 = bf16[1,4096,2048]{2,1,0:T(8,128)(2,1)S(1)} copy-done((bf16[1,4096,2048]{2,1,0:T(8,128)(2,1)S(1)}, bf16[1,4096,2048]{2,1,0:T(8,128)(2,1)}, u32[]{:S(2)}) %copy-start.1) | copy-done | bytes 16777240
  166.7 8.0 %pick_rows.7 = bf16[2,1536,2048]{2,1,0:T(8,128)(2,1)S(1)} custom-call(s32[1]{0:T(128)} %bitcast.8.seq_index, s32[4,8,2,128]{3,2,1,0:T(2,128)S(1)} %bitcast.76, bf16[4,8,128,2048]{3,2,1,0:T(8,128)(2,1)S(1)} %bitcast.71), custom_call_target="tpu_custom_call" | custom-call | flops 1610612736 | bytes 25165824 | tf_op jit(solution)/shard_map/pick_rows/pallas_call | solution.py:166
  179.2 92.9 %all-gather.8.cloned.1.call-done = bf16[4096,2048]{1,0:T(8,128)(2,1)} async-done(((bf16[128,2048]{1,0:T(8,128)(2,1)}), bf16[4096,2048]{1,0:T(8,128)(2,1)}) %all-gather.8.cloned.1.call-update) | async-done | bytes 16777232 | tf_op jit(solution)/shard_map/all_gather | solution.py:299
  272.1 5.8 %copy-done = bf16[4096,2048]{1,0:T(8,128)(2,1)S(1)} copy-done((bf16[4096,2048]{1,0:T(8,128)(2,1)S(1)}, bf16[4096,2048]{1,0:T(8,128)(2,1)}, u32[]{:S(2)}) %copy-start) | copy-done | bytes 16777240
  280.5 6.8 %fusion.40 = f32[2,512,704]{1,2,0:T(8,128)S(1)} fusion(bf16[2,512,2048]{2,1,0:T(8,128)(2,1)S(1)} %pick_rows.4, bf16[2,2048,704]{1,2,0:T(8,128)(2,1)} %param.17), kind=kOutput, calls=%fused_computation.75 | convolution fusion | flops 2952790016 | bytes 12845056 | tf_op jit(solution)/shard_map/erd,edf->erf/dot_general | solution.py:225
  287.4 7.5 %fusion.39 = f32[2,512,704]{1,2,0:T(8,128)} fusion(bf16[2,512,2048]{2,1,0:T(8,128)(2,1)S(1)} %pick_rows.4, bf16[2,2048,704]{1,2,0:T(8,128)(2,1)} %param.16), kind=kOutput, calls=%fused_computation.74 | convolution fusion | flops 2952790016 | bytes 12845056 | tf_op jit(solution)/shard_map/erd,edf->erf/dot_general | solution.py:224
  294.9 7.0 %multiply_reduce_fusion = (f32[2,512]{1,0:T(2,128)}, bf16[2,512,704]{1,2,0:T(8,128)(2,1)S(1)}, bf16[2,512,704]{1,2,0:T(8,128)(2,1)S(1)}, bf16[2,512,704]{1,2,0:T(8,128)(2,1)S(1)}) fusion(f32[2,512,704]{1,2,0:T(8,128)S(1)} %fusion.40, f32[2,512,704]{1,2,0:T(8,128)} %fusion.39, f32[2,512]{1,0:T(2,128)S(1)} %slice-done.4, ...), kind=kOutput, calls=%fused_computation.16 | convolution fusion | flops 2967927808 | bytes 20062208 | tf_op jit(solution)/shard_map/erd,efd->erf/dot_general | solution.py:226
  301.9 7.3 %fusion.41 = f32[2,512,2048]{2,1,0:T(8,128)S(1)} fusion(bf16[2,512,704]{1,2,0:T(8,128)(2,1)S(1)} %get-tuple-element.44, bf16[2,2048,704]{1,2,0:T(8,128)(2,1)} %param.16), kind=kOutput, calls=%fused_computation.76 | convolution fusion | flops 2952790016 | bytes 15597568 | tf_op jit(solution)/shard_map/erf,edf->erd/dot_general | solution.py:316
  309.2 6.6 %add_convert_fusion.rows = bf16[2,512,2048]{2,1,0:T(8,128)(2,1)S(1)} fusion(f32[2,512,2048]{2,1,0:T(8,128)S(1)} %fusion.41, bf16[2,512,704]{1,2,0:T(8,128)(2,1)S(1)} %get-tuple-element.46, bf16[2,2048,704]{1,2,0:T(8,128)(2,1)} %param.17), kind=kOutput, calls=%fused_computation.5 | convolution fusion | flops 2956984320 | bytes 19791872 | tf_op jit(solution)/shard_map/erf,edf->erd/dot_general | solution.py:317
  322.0 16.2 %fusion.42 = f32[2,1536,704]{1,2,0:T(8,128)} fusion(bf16[2,1536,2048]{2,1,0:T(8,128)(2,1)} %copy-done.4, bf16[2,704,2048]{2,1,0:T(8,128)(2,1)} %param.18), kind=kOutput, calls=%fused_computation.77 | convolution fusion | flops 8858370048 | bytes 27000832 | tf_op jit(solution)/shard_map/erd,efd->erf/dot_general | solution.py:226
  338.3 6.5 %convolution_convert_fusion.rows = bf16[2,512,2048]{2,1,0:T(8,128)(2,1)S(1)} fusion(bf16[2,512,704]{1,2,0:T(8,128)(2,1)S(1)} %get-tuple-element.45, bf16[2,704,2048]{2,1,0:T(8,128)(2,1)} %param.18), kind=kOutput, calls=%fused_computation.11 | convolution fusion | flops 2954887168 | bytes 11403264 | tf_op jit(solution)/shard_map/erf,efd->erd/dot_general | solution.py:323
  350.9 8.1 %pick_rows.6 = bf16[2,1536,2048]{2,1,0:T(8,128)(2,1)S(1)} custom-call(s32[1]{0:T(128)} %bitcast.8.seq_index, s32[4,8,2,128]{3,2,1,0:T(2,128)S(1)} %bitcast.78, bf16[4,8,128,2048]{3,2,1,0:T(8,128)(2,1)S(1)} %bitcast.69), custom_call_target="tpu_custom_call" | custom-call | flops 1610612736 | bytes 25165824 | tf_op jit(solution)/shard_map/pick_rows/pallas_call | solution.py:166
  359.0 4.5 copy-done.5
  363.5 16.1 %fusion.44 = f32[2,1536,704]{1,2,0:T(8,128)} fusion(bf16[2,1536,2048]{2,1,0:T(8,128)(2,1)} %copy-done.5, bf16[2,2048,704]{1,2,0:T(8,128)(2,1)} %param.16), kind=kOutput, calls=%fused_computation.79 | convolution fusion | flops 8858370048 | bytes 27000832 | tf_op jit(solution)/shard_map/erd,edf->erf/dot_general | solution.py:224
  380.1 11.6 %fusion.1 = f32[2,512,704]{1,2,0:T(8,128)} fusion(f32[2,1536,704]{1,2,0:T(8,128)} %fusion.42, f32[2,1536]{1,0:T(2,128)S(1)} %slice.29, bf16[2,1536,2048]{2,1,0:T(8,128)(2,1)} %copy-done.5, s32[]{:T(128)S(6)} %select_n.61, f32[2,1536,704]{1,2,0:T(8,128)} %fusion.44), kind=kOutput, calls=%fused_computation.6 | convolution fusion | flops 2229731328 | bytes 23343108 | tf_op jit(solution)/shard_map/erm,ern->emn/dot_general | solution.py:351
  391.7 16.3 %fusion.43 = f32[2,1536,704]{1,2,0:T(8,128)} fusion(bf16[2,1536,2048]{2,1,0:T(8,128)(2,1)} %copy-done.5, bf16[2,2048,704]{1,2,0:T(8,128)(2,1)} %param.17), kind=kOutput, calls=%fused_computation.78 | convolution fusion | flops 8858370048 | bytes 27000832 | tf_op jit(solution)/shard_map/erd,edf->erf/dot_general | solution.py:225
  408.0 9.2 %fusion.5 = f32[2,512,704]{1,2,0:T(8,128)S(1)} fusion(f32[2,1536,704]{1,2,0:T(8,128)S(1)} %bitcast.100, f32[2,1536,704]{1,2,0:T(8,128)} %fusion.43, f32[2,1536,704]{1,2,0:T(8,128)} %fusion.42, f32[2,1536]{1,0:T(2,128)S(1)} %slice.29, bf16[2,1536,2048]{2,1,0:T(8,128)(2,1)} %copy-done.5, s32[]{:T(128)S(6)} %select_n.61), kind=kOutput, calls=%fused_computation.10 | convolution fusion | flops 2238382080 | bytes 31993860 | tf_op jit(solution)/shard_map/erm,ern->emn/dot_general | solution.py:351
  417.2 8.9 %attend_back.1 = (bf16[128,2048]{1,0:T(8,128)(2,1)}, bf16[128,2048]{1,0:T(8,128)(2,1)}, bf16[512,1024]{1,0:T(8,128)(2,1)}) custom-call(bf16[128,2048]{1,0:T(8,128)(2,1)} %bitcast.80, bf16[128,2048]{1,0:T(8,128)(2,1)} %bitcast.83, bf16[512,1024]{1,0:T(8,128)(2,1)} %all-gather.6.cloned.1.call-done.kv, bf16[128,2048]{1,0:T(8,128)(2,1)} %get-tuple-element.16.att, ...), custom_call_target="tpu_custom_call" | custom-call | flops 1342177280 | bytes 5767168 | tf_op jit(solution)/shard_map/attend_back/pallas_call | solution.py:129
  426.1 11.0 %fusion.2 = f32[2,704,512]{2,1,0:T(8,128)} fusion(f32[2,1536,704]{1,2,0:T(8,128)} %fusion.43, f32[2,1536]{1,0:T(2,128)S(1)} %slice.29, bf16[2,1536,2048]{2,1,0:T(8,128)(2,1)} %copy-done.4, s32[]{:T(128)S(6)} %select_n.61, f32[2,1536,704]{1,2,0:T(8,128)} %fusion.44), kind=kOutput, calls=%fused_computation.7 | convolution fusion | flops 2229731328 | bytes 23343108 | tf_op jit(solution)/shard_map/erm,ern->emn/dot_general | solution.py:351
  442.8 4.8 %add_convert_fusion.2 = bf16[2,512,704]{1,2,0:T(8,128)(2,1)} fusion(f32[2,512,704]{1,2,0:T(8,128)} %fusion.1, bf16[2,512,704]{1,2,0:T(8,128)(2,1)} %copy-done.15, bf16[2,512,2048]{2,1,0:T(8,128)(2,1)} %copy-done.6, s32[]{:T(128)S(6)} %select_n.61), kind=kOutput, calls=%fused_computation.14 | convolution fusion | flops 739639296 | bytes 6815748 | tf_op jit(solution)/shard_map/erm,ern->emn/dot_general | solution.py:350
  (108 shorter events, 49.1 us)
Async XLA Ops:
  7.2 30.9 %all-gather.6.cloned.1.call-start = ((), (), s32[]{:S(2)}) async-start(), calls=%async_computation.4 | async-start | bytes 1310720 | tf_op jit(solution)/shard_map/all_gather | solution.py:268
  8.9 147.1 %all-gather.10.cloned.1.call-start = ((), (), s32[]{:S(2)}) async-start(), calls=%async_computation.9 | async-start | bytes 17301504 | tf_op jit(solution)/shard_map/all_gather | solution.py:287
  9.7 262.4 %all-gather.8.cloned.1.call-start = ((), (), s32[]{:S(2)}) async-start(), calls=%async_computation.5 | async-start | bytes 17301504 | tf_op jit(solution)/shard_map/all_gather | solution.py:299
  42.8 374.5 %reduce-scatter.6.cloned.1.call-start = ((), (), s32[]{:S(2)}) async-start(), calls=%async_computation.7 | async-start | bytes 4718592 | tf_op jit(solution)/shard_map/reduce_scatter | solution.py:321
  43.5 33.3 %copy-start.17 = (s32[1,128,6]{1,2,0:T(8,128)}, s32[1,128,6]{1,2,0:T(8,128)S(1)}, u32[]{:S(2)}) copy-start(s32[1,128,6]{1,2,0:T(8,128)S(1)} %copy.51) | copy-start | bytes 9220
  78.3 86.4 %copy-start.16 = (f32[2,2048]{1,0:T(2,128)}, f32[2,2048]{1,0:T(2,128)S(1)}, u32[]{:S(2)}) copy-start(f32[2,2048]{1,0:T(2,128)S(1)} %reshape.109) | copy-start | bytes 49156
  280.5 14.4 %slice-start.5 = ((s8[5767168]{0:T(1024)(128)(4,1)}), s8[4194304]{0:T(1024)(128)(4,1)S(1)}, s32[]{:S(2)}) async-start(s8[5767168]{0:T(1024)(128)(4,1)} %bitcast.95), calls=%async_computation.15 | async-start | bytes 8388608
  287.3 7.5 %copy-start.8 = (bf16[2,512,2048]{2,1,0:T(8,128)(2,1)S(1)}, bf16[2,512,2048]{2,1,0:T(8,128)(2,1)}, u32[]{:S(2)}) copy-start(bf16[2,512,2048]{2,1,0:T(8,128)(2,1)} %copy-done.7) | copy-start | bytes 12582916
  287.3 7.5 %slice-start.4 = ((f32[2,2048]{1,0:T(2,128)}), f32[2,512]{1,0:T(2,128)S(1)}, s32[]{:S(2)}) async-start(f32[2,2048]{1,0:T(2,128)} %copy-done.16), calls=%async_computation.14 | async-start | bytes 8192 | tf_op jit(solution)/shard_map/slice | solution.py:313
  287.4 7.5 %slice-start.6 = ((s8[5767168]{0:T(1024)(128)(4,1)}), s8[1572864]{0:T(1024)(128)(4,1)S(1)}, s32[]{:S(2)}) async-start(s8[5767168]{0:T(1024)(128)(4,1)} %bitcast.95), calls=%async_computation.16 | async-start | bytes 3145728
  301.9 7.3 %copy-start.11 = (bf16[2,512,704]{1,2,0:T(8,128)(2,1)}, bf16[2,512,704]{1,2,0:T(8,128)(2,1)S(1)}, u32[]{:S(2)}) copy-start(bf16[2,512,704]{1,2,0:T(8,128)(2,1)S(1)} %get-tuple-element.44) | copy-start | bytes 4325380
  301.9 7.3 %copy-start.15 = (bf16[2,512,704]{1,2,0:T(8,128)(2,1)}, bf16[2,512,704]{1,2,0:T(8,128)(2,1)S(1)}, u32[]{:S(2)}) copy-start(bf16[2,512,704]{1,2,0:T(8,128)(2,1)S(1)} %get-tuple-element.46) | copy-start | bytes 4325380
  301.9 36.4 %copy-start.13 = (bf16[2,512,704]{1,2,0:T(8,128)(2,1)}, bf16[2,512,704]{1,2,0:T(8,128)(2,1)S(1)}, u32[]{:S(2)}) copy-start(bf16[2,512,704]{1,2,0:T(8,128)(2,1)S(1)} %get-tuple-element.45) | copy-start | bytes 4325380
  322.0 132.9 %reduce-scatter.4.cloned.1.call-start = ((), (), s32[]{:S(2)}) async-start(), calls=%async_computation.6 | async-start | bytes 4718592 | tf_op jit(solution)/shard_map/reduce_scatter | solution.py:327
  322.0 28.9 %slice-start = ((s8[16777216]{0:T(1024)(128)(4,1)}), s8[4194304]{0:T(1024)(128)(4,1)S(1)}, s32[]{:S(2)}) async-start(s8[16777216]{0:T(1024)(128)(4,1)} %bitcast.67), calls=%async_computation.10 | async-start | bytes 8388608
  322.0 28.9 %slice-start.1 = ((s8[16777216]{0:T(1024)(128)(4,1)}), s8[4194304]{0:T(1024)(128)(4,1)S(1)}, s32[]{:S(2)}) async-start(s8[16777216]{0:T(1024)(128)(4,1)} %bitcast.67), calls=%async_computation.11 | async-start | bytes 8388608
  322.0 28.8 %slice-start.2 = ((s8[16777216]{0:T(1024)(128)(4,1)}), s8[4194304]{0:T(1024)(128)(4,1)S(1)}, s32[]{:S(2)}) async-start(s8[16777216]{0:T(1024)(128)(4,1)} %bitcast.67), calls=%async_computation.12 | async-start | bytes 8388608
  338.3 12.6 %slice-start.3 = ((s8[16777216]{0:T(1024)(128)(4,1)}), s8[4194304]{0:T(1024)(128)(4,1)S(1)}, s32[]{:S(2)}) async-start(s8[16777216]{0:T(1024)(128)(4,1)} %bitcast.67), calls=%async_computation.13 | async-start | bytes 8388608
  379.6 78.4 %reduce-scatter.8.cloned.1.call-start = ((), (), s32[]{:S(2)}) async-start(), calls=%async_computation.8 | async-start | bytes 1310720 | tf_op jit(solution)/shard_map/reduce_scatter | solution.py:362
  380.1 27.9 %slice-start.7 = ((s8[8650752]{0:T(1024)(128)(4,1)}), s8[262144]{0:T(1024)(128)(4,1)S(1)}, s32[]{:S(2)}) async-start(s8[8650752]{0:T(1024)(128)(4,1)} %bitcast.99), calls=%async_computation.17 | async-start | bytes 524288
  380.1 27.9 %slice-start.8 = ((s8[8650752]{0:T(1024)(128)(4,1)}), s8[4194304]{0:T(1024)(128)(4,1)S(1)}, s32[]{:S(2)}) async-start(s8[8650752]{0:T(1024)(128)(4,1)} %bitcast.99), calls=%async_computation.18 | async-start | bytes 8388608
  391.7 16.3 %slice-start.9 = ((s8[8650752]{0:T(1024)(128)(4,1)}), s8[4194304]{0:T(1024)(128)(4,1)S(1)}, s32[]{:S(2)}) async-start(s8[8650752]{0:T(1024)(128)(4,1)} %bitcast.99), calls=%async_computation.19 | async-start | bytes 8388608
  426.1 11.0 %copy-start.19 = (f32[2,512]{1,0:T(2,128)S(1)}, f32[2,512]{1,0:T(2,128)}, u32[]{:S(2)}) copy-start(f32[2,512]{1,0:T(2,128)} %get-tuple-element.43) | copy-start | bytes 12292
  439.0 15.3 %all-to-all-start = ((f32[8,2,128]{2,1,0:T(2,128)}), f32[8,2,128]{2,1,0:T(2,128)S(1)}, u32[]{:S(2)}, u32[]{:S(2)}) async-start(f32[8,2,128]{2,1,0:T(2,128)} %select_reduce_fusion.1), calls=%async_computation.3 | async-start | bytes 16384 | tf_op jit(solution)/shard_map/all_to_all | solution.py:336
  (13 other events, 53.5 us)
Sparse Core Ops, SparseCore 0:
  10.1 27.9 all-gather.5
  41.0 115.0 all-gather.9
  159.5 112.5 all-gather.7
  322.1 49.9 reduce-scatter.5
  379.7 50.1 reduce-scatter.3
  432.1 25.9 reduce-scatter.7
where the time goes:
time: 474 us; the launch traced here: 467 us
  waiting for transfers between devices  200 us (42%)
  matrix products  134 us (28%)
  Pallas kernels  43.3 us (9%)
  blocking collectives  32.6 us (7%)
  local copies, waits for them, and re-layouts  30.5 us (6%)
  between operations  14.8 us (3%)
  other arithmetic  7.95 us (2%)
    all_gather x1, waiting for transfers between devices, on_device(): normed_all = lax.all_gather(normed_bf, both, axis=0, tiled=True)  92.9 us
    all_gather x1, waiting for transfers between devices, on_device(): grads_all = lax.all_gather(grad_rows, both, axis=0, tiled=True)  76.6 us
    all_gather x1, blocking collectives, on_device(): tables = lax.all_gather(table, both, axis=0, tiled=False)  32.6 us
    dot_general x3, matrix products, outer(): jnp.einsum('erm,ern->emn', a_far, b_far, preferred_element_type=F32)  31.8 us
    unnamed x62, local copies, waits for them, and re-layouts  28.6 us
    all_gather x1, waiting for transfers between devices, on_device(): kv = lax.all_gather(kv_mine, 'seq', axis=0, tiled=True)  28.4 us
    dot_general x2, matrix products, hidden_units(): jnp.einsum('erd,edf->erf', rows, gate_weight, preferred_element_type=F32)  23.6 us
    dot_general x2, matrix products, hidden_units(): jnp.einsum('erd,efd->erf', grads, down_weight, preferred_element_type=F32)  23.2 us
  transfers between devices with their start and end apart: 7, of which 4 were waited for; matrix products, arithmetic and copies ran while one was open for 23% of the time, Pallas kernels for 8%

commit v1 on v0

--- a/solution.py
+++ b/solution.py
@@ -14,6 +14,7 @@
 BF = jnp.bfloat16
 F32 = jnp.float32
 GATHER_BYTES = 32 * 1024 * 1024
+MESH = pl.DeviceIdType.MESH
 VMEM_LIMIT = 56 * 1024 * 1024
 
 
@@ -85,6 +86,323 @@
         ),
         name="attend",
     )(residual, q, kv)
+
+
+def attend_rows(group, residual, q, kv, att, log_total, inv_rms, normed):
+    tokens = q.shape[0]
+    full = kv.shape[0]
+    kv_heads = kv.shape[1] // (2 * DH)
+    visible = visible_mask(tokens, group, full, lax.axis_index("seq"))
+    scale = 1.0 / math.sqrt(DH)
+    for k in range(kv_heads):
+        qh = heads_of(q, k * group, group)
+        kh = kv[:, k * DH : (k + 1) * DH]
+        vh = kv[:, (kv_heads + k) * DH : (kv_heads + k + 1) * DH]
+        scores = jnp.where(visible, dot(qh, kh, 1, 1) * scale, neg_big)
+        top = jnp.max(scores, axis=1, keepdims=True)
+        weights = jnp.exp(scores - top)
+        total = jnp.sum(weights, axis=1, keepdims=True)
+        out = (dot(weights.astype(BF), vh, 1, 0) / total).astype(BF)
+        logs = top + jnp.log(total)
+        for g in range(group):
+            h = k * group + g
+            att[:, h * DH : (h + 1) * DH] = out[g * tokens : (g + 1) * tokens]
+            log_total[:, h : h + 1] = logs[g * tokens : (g + 1) * tokens]
+    hidden = residual[...].astype(F32) + att[...].astype(F32)
+    inv = lax.rsqrt(jnp.mean(hidden * hidden, axis=1, keepdims=True) + norm_eps)
+    inv_rms[...] = inv
+    normed[...] = (hidden * inv).astype(BF)
+
+
+def front_kernel(
+    group,
+    seqs,
+    residual,
+    q,
+    kv_mine,
+    table,
+    grads,
+    att,
+    log_total,
+    inv_rms,
+    kv_all,
+    grads_all,
+    normed_all,
+    tables,
+    kv,
+    normed,
+    local_sem,
+    kv_sem,
+    line_sem,
+    plane_sem,
+    table_line_sem,
+    table_plane_sem,
+):
+    z = lax.axis_index("seq")
+    e = lax.axis_index("expert")
+    c, x, y = lax.rem(e, 2), lax.rem(e // 2, 2), e // 4
+    tokens = q.shape[0]
+    half = tokens // 2
+    sibling = {"expert": e + 1 - 2 * c}
+    across_x = {"expert": e + 2 - 4 * x}
+    across_y = {"expert": e + 4 - 8 * y}
+    above, below = {"seq": z + 1}, {"seq": z - 1}
+    top = seqs - 1
+    arrays = (grads_all, normed_all)
+    sends = []
+
+    def copy_of(view, sems, device):
+        return pltpu.make_async_remote_copy(
+            src_ref=view,
+            dst_ref=view,
+            send_sem=sems.at[0],
+            recv_sem=sems.at[1],
+            device_id=device,
+            device_id_type=MESH,
+        )
+
+    def send(guard, view, sems, device):
+        copy_of(view(), sems(), device).start()
+        sends.append((guard, lambda: copy_of(view(), sems(), device).wait_send()))
+
+    def arrived(view, sems):
+        copy_of(view, sems, sibling).wait_recv()
+
+    def under(guard, body):
+        if guard is True:
+            body()
+        else:
+            pl.when(guard)(body)
+
+    def plane(k):
+        d = (k + 1) // 2
+        return z if k == 0 else (z - d if k % 2 else z + d)
+
+    def present(k):
+        d = (k + 1) // 2
+        return True if k == 0 else (z >= d if k % 2 else z + d <= top)
+
+    def forwarded(k):
+        d = (k + 1) // 2
+        return z + 1 <= top if k % 2 else z >= 1
+
+    def both(a, b):
+        return b if a is True else (a if b is True else jnp.logical_and(a, b))
+
+    def line_start(ref, sems, k):
+        guard = both(present(k - 2) if k > 2 else True, forwarded(k))
+
+        def block():
+            return ref.at[plane(k - 2) if k > 2 else z, y, x, c]
+
+        under(guard, lambda: send(guard, block, lambda: sems(k), above if k % 2 else below))
+
+    def first(a, k):
+        ref = arrays[a]
+
+        def sems(i):
+            return plane_sem.at[a, k, i]
+
+        if k:
+
+            def take():
+                arrived(ref.at[plane(k), y, x, c], line_sem.at[a, k])
+                if a == 0:
+                    arrived(tables.at[plane(k), y, x, c], table_line_sem.at[k])
+
+            under(present(k), take)
+            if k + 2 <= 2 * top:
+                line_start(ref, lambda j: line_sem.at[a, j], k + 2)
+                if a == 0:
+                    line_start(tables, lambda j: table_line_sem.at[j], k + 2)
+
+        def start():
+            send(k, lambda: ref.at[plane(k), y, x, c, :half], lambda: sems(0), across_x)
+            send(k, lambda: ref.at[plane(k), y, x, c, half:], lambda: sems(1), across_y)
+            if a == 0:
+                send(
+                    k,
+                    lambda: tables.at[plane(k), y, x, c],
+                    lambda: table_plane_sem.at[k, 0],
+                    across_x,
+                )
+
+        under(present(k), start)
+
+    def second(a, k):
+        ref = arrays[a]
+
+        def sems(i):
+            return plane_sem.at[a, k, i]
+
+        def step():
+            p = plane(k)
+            arrived(ref.at[p, y, 1 - x, c, :half], sems(0))
+            send(k, lambda: ref.at[plane(k), y, :, c, :half], lambda: sems(2), across_y)
+            arrived(ref.at[p, 1 - y, x, c, half:], sems(1))
+            send(k, lambda: ref.at[plane(k), :, x, c, half:], lambda: sems(3), across_x)
+            if a == 0:
+                arrived(tables.at[p, y, 1 - x, c], table_plane_sem.at[k, 0])
+                send(
+                    k,
+                    lambda: tables.at[plane(k), y, :, c],
+                    lambda: table_plane_sem.at[k, 1],
+                    across_y,
+                )
+
+        under(present(k), step)
+
+    def third(a, k):
+        ref = arrays[a]
+
+        def sems(i):
+            return plane_sem.at[a, k, i]
+
+        def step():
+            p = plane(k)
+            arrived(ref.at[p, 1 - y, :, c, :half], sems(2))
+            arrived(ref.at[p, :, 1 - x, c, half:], sems(3))
+            send(k, lambda: ref.at[plane(k), :, :, c], lambda: sems(4), sibling)
+            if a == 0:
+                arrived(tables.at[p, 1 - y, :, c], table_plane_sem.at[k, 1])
+                send(
+                    k,
+                    lambda: tables.at[plane(k), :, :, c],
+                    lambda: table_plane_sem.at[k, 2],
+                    sibling,
+                )
+
+        under(present(k), step)
+
+    def fourth(a, k):
+        def step():
+            p = plane(k)
+            arrived(arrays[a].at[p, :, :, 1 - c], plane_sem.at[a, k, 4])
+            if a == 0:
+                arrived(tables.at[p, :, :, 1 - c], table_plane_sem.at[k, 2])
+
+        under(present(k), step)
+
+    copies = [
+        pltpu.make_async_copy(grads, grads_all.at[z, y, x, c], local_sem.at[0]),
+        pltpu.make_async_copy(table, tables.at[z, y, x, c], local_sem.at[1]),
+        pltpu.make_async_copy(kv_mine, kv.at[z], local_sem.at[2]),
+    ]
+    for copy in copies:
+        copy.start()
+    for j in range(1, seqs):
+
+        @pl.when(j > z)
+        def _():
+            kv[j] = jnp.zeros(kv.shape[1:], BF)
+
+    barrier = pltpu.get_barrier_semaphore()
+    for device in (sibling, across_x, across_y):
+        pl.semaphore_signal(barrier, inc=1, device_id=device, device_id_type=MESH)
+
+    @pl.when(z < top)
+    def _():
+        pl.semaphore_signal(barrier, inc=1, device_id=above, device_id_type=MESH)
+
+    @pl.when(z > 0)
+    def _():
+        pl.semaphore_signal(barrier, inc=1, device_id=below, device_id_type=MESH)
+
+    pl.semaphore_wait(barrier, 3 + (z < top).astype(jnp.int32) + (z > 0).astype(jnp.int32))
+    for copy in copies:
+        copy.wait()
+
+    def kv_start(d):
+        guard = both(z >= d if d else True, z < top)
+        under(guard, lambda: send(guard, lambda: kv.at[z - d], lambda: kv_sem.at[d + 1], above))
+
+    def kv_take(d):
+        @pl.when(z >= d)
+        def _():
+            arrived(kv.at[z - d], kv_sem.at[d])
+
+    kv_start(0)
+    line_start(grads_all, lambda j: line_sem.at[0, j], 2)
+    line_start(tables, lambda j: table_line_sem.at[j], 2)
+    line_start(tables, lambda j: table_line_sem.at[j], 1)
+    first(0, 0)
+    for d in range(1, seqs):
+        kv_take(d)
+        if d < top:
+            kv_start(d)
+        if d == 1:
+            second(0, 0)
+        if d == 2:
+            third(0, 0)
+    line_start(grads_all, lambda j: line_sem.at[0, j], 1)
+    keys = kv[...].reshape(seqs * tokens, kv.shape[2])
+    attend_rows(group, residual, q, keys, att, log_total, inv_rms, normed)
+    keep = [
+        pltpu.make_async_copy(normed, normed_all.at[z, y, x, c], local_sem.at[3]),
+        pltpu.make_async_copy(kv, kv_all, local_sem.at[4]),
+    ]
+    for copy in keep:
+        copy.start()
+    keep[0].wait()
+    line_start(normed_all, lambda j: line_sem.at[1, j], 1)
+    line_start(normed_all, lambda j: line_sem.at[1, j], 2)
+    order = [(1, 0)]
+    for d in range(1, seqs):
+        for a in range(2):
+            order += [(a, 2 * d - 1), (a, 2 * d)]
+    for i in range(len(order) + 4):
+        if i < len(order):
+            first(*order[i])
+        if 0 <= i - 2 < len(order):
+            second(*order[i - 2])
+        if 0 <= i - 4 < len(order):
+            third(*order[i - 4])
+    keep[1].wait()
+    for a, k in [(0, 0)] + order:
+        fourth(a, k)
+    for guard, finish in sends:
+        under(present(guard) if isinstance(guard, int) else guard, finish)
+
+
+def front(residual, q, kv_mine, table, grads, group, seqs):
+    tokens, width = q.shape
+    heads = width // DH
+    slots = 2 * seqs - 1
+    any_space = pl.BlockSpec(memory_space=pl.ANY)
+    dma = pltpu.SemaphoreType.DMA
+    return pl.pallas_call(
+        functools.partial(front_kernel, group, seqs),
+        out_shape=(
+            jax.ShapeDtypeStruct((tokens, width), BF),
+            jax.ShapeDtypeStruct((tokens, heads), F32),
+            jax.ShapeDtypeStruct((tokens, 1), F32),
+            jax.ShapeDtypeStruct((seqs,) + kv_mine.shape, BF),
+            jax.ShapeDtypeStruct((seqs, 2, 2, 2, tokens, width), BF),
+            jax.ShapeDtypeStruct((seqs, 2, 2, 2, tokens, width), BF),
+            jax.ShapeDtypeStruct((seqs, 2, 2, 2) + table.shape, F32),
+        ),
+        in_specs=[vm()] * 5,
+        out_specs=(vm(),) * 3 + (any_space,) * 4,
+        scratch_shapes=[
+            pltpu.VMEM((seqs,) + kv_mine.shape, BF),
+            pltpu.VMEM((tokens, width), BF),
+            dma((5,)),
+            dma((seqs, 2)),
+            dma((2, slots, 2)),
+            dma((2, slots, 5, 2)),
+            dma((slots, 2)),
+            dma((slots, 3, 2)),
+        ],
+        compiler_params=pltpu.CompilerParams(
+            collective_id=0, has_side_effects=True, vmem_limit_bytes=VMEM_LIMIT
+        ),
+        cost_estimate=pl.CostEstimate(
+            flops=4 * tokens * seqs * tokens * width,
+            bytes_accessed=32 * seqs * tokens * width,
+            transcendentals=heads * tokens * seqs * tokens,
+        ),
+        name="front",
+    )(residual, q, kv_mine, table, grads)
 
 
 def attend_back_kernel(
@@ -258,6 +576,7 @@
     capacity = tokens * top_count * 5 // (4 * experts)
     depth = -(-capacity // 16) * 16
     both = ("seq", "expert")
+    both_size = seqs * ranks
     seq_index = lax.axis_index("seq")
     rank_index = lax.axis_index("expert")
     seq_array = seq_index.astype(jnp.int32).reshape(1)
@@ -265,8 +584,6 @@
     kv_mine = jnp.concatenate(
         [key_input.reshape(tokens, kv_width), value_input.reshape(tokens, kv_width)], axis=1
     )
-    kv = lax.all_gather(kv_mine, "seq", axis=0, tiled=True)
-
     expert_ids = jnp.arange(experts, dtype=jnp.int32)
     picked = routes.reshape(tokens, top_count)
     mix_rows = mix_weights.reshape(tokens, top_count)
@@ -274,7 +591,24 @@
     table = jnp.sum(jnp.where(hit, mix_rows[None], 0.0), axis=2) - (
         1.0 - jnp.sum(hit.astype(F32), axis=2)
     )
-    tables = lax.all_gather(table, both, axis=0, tiled=False)
+    grad_rows = grad_out.reshape(tokens, width)
+    q = queries.reshape(tokens, width)
+    res = residual.reshape(tokens, width)
+    paired = ranks == 8 and 2 * both_size * grad_rows.size <= GATHER_BYTES
+    if paired:
+        att, log_total, inv_rms, kv, grads_all, normed_all, tables = front(
+            res, q, kv_mine, table, grad_rows, group, seqs
+        )
+        kv = kv.reshape(seqs * tokens, 2 * kv_width)
+        grads_all = grads_all.reshape(seqs, ranks, tokens, width)
+        normed_all = normed_all.reshape(seqs, ranks, tokens, width)
+        tables = tables.reshape(seqs * ranks, experts, tokens)
+    else:
+        kv = lax.all_gather(kv_mine, "seq", axis=0, tiled=True)
+        tables = lax.all_gather(table, both, axis=0, tiled=False)
+        grads_all = lax.all_gather(grad_rows, both, axis=0, tiled=True)
+        grads_all = grads_all.reshape(seqs, ranks, tokens, width)
+        att, log_total, inv_rms, normed_bf = attend(res, q, kv, group)
     mine = lax.dynamic_slice_in_dim(tables, rank_index * local, local, axis=1)
     routed = mine >= 0.0
     before = jnp.triu(jnp.ones((tokens, tokens), BF), 1)
@@ -283,21 +617,14 @@
     slot = slot.reshape(seqs, ranks, local, tokens)
     mine = mine.reshape(seqs, ranks, local, tokens)
 
-    grad_rows = grad_out.reshape(tokens, width)
-    grads_all = lax.all_gather(grad_rows, both, axis=0, tiled=True)
-    grads_all = grads_all.reshape(seqs, ranks, tokens, width)
-
-    q = queries.reshape(tokens, width)
-    res = residual.reshape(tokens, width)
-    att, log_total, inv_rms, normed_bf = attend(res, q, kv, group)
     grads_own = pick_rows(grads_all, slot, seq_array, 0, 1, depth)
     grads_far = pick_rows(grads_all, slot, seq_array, 1, seqs - 1, depth)
-    if 2 * grads_all.size > GATHER_BYTES:
+    if not paired:
         normed_bf, grads_own, grads_far = lax.optimization_barrier(
             (normed_bf, grads_own, grads_far)
         )
-    normed_all = lax.all_gather(normed_bf, both, axis=0, tiled=True)
-    normed_all = normed_all.reshape(seqs, ranks, tokens, width)
+        normed_all = lax.all_gather(normed_bf, both, axis=0, tiled=True)
+        normed_all = normed_all.reshape(seqs, ranks, tokens, width)
 
     slot_turned = jnp.roll(slot, -seq_index, axis=0)
     mix_turned = jnp.roll(mine, -seq_index, axis=0)

time: 474 us -> 396 us (0.84)
  waiting for transfers between devices: 200 us -> 3.04 us
  Pallas kernels: 43.3 us -> 195 us
  blocking collectives: 32.6 us -> 0 us
  local copies, waits for them, and re-layouts: 30.5 us -> 35.9 us
    all_gather x3 -> x0, waiting for transfers between devices: 198 us -> none  [the longest x1 92.9 us: on_device(): normed_all = lax.all_gather(normed_bf, both, axis=0, tiled=True)]
    pallas_call x1, Pallas kernels: 4.62 us -> 156 us  [front(): pl.pallas_call(functools.partial(front_kernel, group, seqs), out_shape=(j...]
    all_gather x1 -> x0, blocking collectives: 32.6 us -> none  [on_device(): tables = lax.all_gather(table, both, axis=0, tiled=False)]
    unnamed x62 -> x64, local copies, waits for them, and re-layouts: 28.6 us -> 33 us
  transfers between devices with their start and end apart: 7 -> 4, of which waited for: 4 -> 1; matrix products, arithmetic and copies ran while one was open for 23% -> 25% of each run, Pallas kernels for 8% -> 7%
where the time goes in v1:
time: 396 us; the launch traced here: 388 us
  Pallas kernels  195 us (49%)
  matrix products  130 us (33%)
  local copies, waits for them, and re-layouts  35.9 us (9%)
  between operations  14.4 us (4%)
  other arithmetic  6.84 us (2%)
    pallas_call x1, Pallas kernels, front(): pl.pallas_call(functools.partial(front_kernel, group, seqs), out_shape=(j...  156 us
    unnamed x64, local copies, waits for them, and re-layouts  33 us
    dot_general x3, matrix products, outer(): jnp.einsum('erm,ern->emn', a_far, b_far, preferred_element_type=F32)  31 us
    dot_general x2, matrix products, hidden_units(): jnp.einsum('erd,edf->erf', rows, gate_weight, preferred_element_type=F32)  23.6 us
    dot_general x2, matrix products, hidden_units(): jnp.einsum('erd,efd->erf', grads, down_weight, preferred_element_type=F32)  23.2 us
    pallas_call x4, Pallas kernels, pick_rows(): pl.pallas_call(pick_kernel, out_shape=jax.ShapeDtypeStruct((local, count...  21.5 us
    dot_general x2, matrix products, hidden_units(): jnp.einsum('erd,edf->erf', rows, up_weight, preferred_element_type=F32)  21.3 us
    dot_general x3, matrix products, outer(): jnp.einsum('erm,ern->emn', a_own, b_own, preferred_element_type=F32)  9.83 us
  transfers between devices with their start and end apart: 4, of which 1 were waited for; matrix products, arithmetic and copies ran while one was open for 25% of the time, Pallas kernels for 7%

profile of v1, /device:TPU:19, one launch (start us, length us, event | category | flops | bytes accessed | tf_op | source)
XLA Modules:
  0.0 388.3 jit_solution(288543673550074343)
XLA Ops:
  10.9 155.7 %front.1 = (bf16[128,2048]{1,0:T(8,128)(2,1)}, f32[128,16]{1,0:T(8,128)}, f32[128,1]{1,0:T(8,128)}, bf16[4,128,1024]{2,1,0:T(8,128)(2,1)}, bf16[4,2,2,2,128,2048...) custom-call(bf16[128,2048]{1,0:T(8,128)(2,1)} %bitcast.80, ...), custom_call_target="tpu_custom_call" | custom-call | flops 536870912 | bytes 33554432 | tf_op jit(solution)/shard_map/front/pallas_call | solution.py:373
  169.1 5.8 %copy-done.1 = bf16[4,2,2,2,128,2048]{5,4,3,2,1,0:T(8,128)(2,1)S(1)} copy-done((bf16[4,2,2,2,128,2048]{5,4,3,2,1,0:T(8,128)(2,1)S(1)}, bf16[4,2,2,2,128,2048]{5,4,3,2,1,0:T(8,128)(2,1)}, u32[]{:S(2)}) %copy-start.1) | copy-done | bytes 16777240
  177.7 4.7 %fusion.40 = f32[2,512,704]{1,2,0:T(8,128)} fusion(bf16[2,512,2048]{2,1,0:T(8,128)(2,1)S(1)} %pick_rows.4, bf16[2,2048,704]{1,2,0:T(8,128)(2,1)S(1)} %copy-done.22), kind=kOutput, calls=%fused_computation.75 | convolution fusion | flops 2952790016 | bytes 12845056 | tf_op jit(solution)/shard_map/erd,edf->erf/dot_general | solution.py:543
  182.4 7.6 %fusion.39 = f32[2,512,704]{1,2,0:T(8,128)} fusion(bf16[2,512,2048]{2,1,0:T(8,128)(2,1)S(1)} %pick_rows.4, bf16[2,2048,704]{1,2,0:T(8,128)(2,1)} %param.16), kind=kOutput, calls=%fused_computation.74 | convolution fusion | flops 2952790016 | bytes 12845056 | tf_op jit(solution)/shard_map/erd,edf->erf/dot_general | solution.py:542
  192.8 9.9 %multiply_reduce_fusion = (f32[2,512]{1,0:T(2,128)S(1)}, bf16[2,512,704]{1,2,0:T(8,128)(2,1)S(1)}, bf16[2,512,704]{1,2,0:T(8,128)(2,1)S(1)}, bf16[2,512,704]{1,2,0:T(8,128)(2,1)S(1)}) fusion(f32[2,512,704]{1,2,0:T(8,128)} %fusion.40, f32[2,512,704]{1,2,0:T(8,128)} %fusion.39, f32[2,512]{1,0:T(2,128)S(1)} %slice-done.4, ...), kind=kOutput, calls=%fused_computation.16 | convolution fusion | flops 2967927808 | bytes 20062208 | tf_op jit(solution)/shard_map/erd,efd->erf/dot_general | solution.py:544
  202.8 7.3 %fusion.41 = f32[2,512,2048]{2,1,0:T(8,128)S(1)} fusion(bf16[2,512,704]{1,2,0:T(8,128)(2,1)S(1)} %get-tuple-element.50, bf16[2,2048,704]{1,2,0:T(8,128)(2,1)} %param.16), kind=kOutput, calls=%fused_computation.76 | convolution fusion | flops 2952790016 | bytes 15597568 | tf_op jit(solution)/shard_map/erf,edf->erd/dot_general | solution.py:643
  210.1 6.5 %add_convert_fusion.rows = bf16[2,512,2048]{2,1,0:T(8,128)(2,1)S(1)} fusion(f32[2,512,2048]{2,1,0:T(8,128)S(1)} %fusion.41, bf16[2,512,704]{1,2,0:T(8,128)(2,1)S(1)} %get-tuple-element.52, bf16[2,2048,704]{1,2,0:T(8,128)(2,1)} %param.17), kind=kOutput, calls=%fused_computation.5 | convolution fusion | flops 2956984320 | bytes 19791872 | tf_op jit(solution)/shard_map/erf,edf->erd/dot_general | solution.py:644
  216.6 4.5 %spread_rows.3 = bf16[8,128,2048]{2,1,0:T(8,128)(2,1)S(1)} custom-call(s32[8,2,128]{2,1,0:T(2,128)S(1)} %slice_bitcast_fusion.3.slot, bf16[2,512,2048]{2,1,0:T(8,128)(2,1)S(1)} %add_convert_fusion.rows), custom_call_target="tpu_custom_call" | custom-call | flops 536870912 | bytes 8388608 | tf_op jit(solution)/shard_map/spread_rows/pallas_call | solution.py:522
  228.2 6.8 %convolution_convert_fusion.rows = bf16[2,512,2048]{2,1,0:T(8,128)(2,1)S(1)} fusion(bf16[2,512,704]{1,2,0:T(8,128)(2,1)S(1)} %get-tuple-element.51, bf16[2,704,2048]{2,1,0:T(8,128)(2,1)} %param.18), kind=kOutput, calls=%fused_computation.11 | convolution fusion | flops 2954887168 | bytes 11403264 | tf_op jit(solution)/shard_map/erf,efd->erd/dot_general | solution.py:650
  235.0 4.1 %spread_rows.2 = bf16[8,128,2048]{2,1,0:T(8,128)(2,1)S(1)} custom-call(s32[8,2,128]{2,1,0:T(2,128)S(1)} %slice_bitcast_fusion.3.slot, bf16[2,512,2048]{2,1,0:T(8,128)(2,1)S(1)} %convolution_convert_fusion.rows), custom_call_target="tpu_custom_call" | custom-call | flops 536870912 | bytes 8388608 | tf_op jit(solution)/shard_map/spread_rows/pallas_call | solution.py:522
  241.2 6.4 %copy-done.2 = bf16[4,2,2,2,128,2048]{5,4,3,2,1,0:T(8,128)(2,1)S(1)} copy-done((bf16[4,2,2,2,128,2048]{5,4,3,2,1,0:T(8,128)(2,1)S(1)}, bf16[4,2,2,2,128,2048]{5,4,3,2,1,0:T(8,128)(2,1)}, u32[]{:S(2)}) %copy-start.2) | copy-done | bytes 16777240
  247.6 8.0 %pick_rows.6 = bf16[2,1536,2048]{2,1,0:T(8,128)(2,1)S(1)} custom-call(s32[1]{0:T(128)} %bitcast.9.seq_index, s32[4,8,2,128]{3,2,1,0:T(2,128)S(1)} %bitcast.78, bf16[4,8,128,2048]{3,2,1,0:T(8,128)(2,1)S(1)} %bitcast.72), custom_call_target="tpu_custom_call" | custom-call | flops 1610612736 | bytes 25165824 | tf_op jit(solution)/shard_map/pick_rows/pallas_call | solution.py:484
  255.6 4.5 %copy-done.7 = bf16[2,1536,2048]{2,1,0:T(8,128)(2,1)} copy-done((bf16[2,1536,2048]{2,1,0:T(8,128)(2,1)}, bf16[2,1536,2048]{2,1,0:T(8,128)(2,1)S(1)}, u32[]{:S(2)}) %copy-start.7) | copy-done | bytes 12582936
  260.1 5.8 %copy-done = bf16[4,2,2,2,128,2048]{5,4,3,2,1,0:T(8,128)(2,1)S(1)} copy-done((bf16[4,2,2,2,128,2048]{5,4,3,2,1,0:T(8,128)(2,1)S(1)}, bf16[4,2,2,2,128,2048]{5,4,3,2,1,0:T(8,128)(2,1)}, u32[]{:S(2)}) %copy-start) | copy-done | bytes 16777240
  265.9 8.0 %pick_rows.7 = bf16[2,1536,2048]{2,1,0:T(8,128)(2,1)S(1)} custom-call(s32[1]{0:T(128)} %bitcast.9.seq_index, s32[4,8,2,128]{3,2,1,0:T(2,128)S(1)} %bitcast.79, bf16[4,8,128,2048]{3,2,1,0:T(8,128)(2,1)S(1)} %bitcast.70), custom_call_target="tpu_custom_call" | custom-call | flops 1610612736 | bytes 25165824 | tf_op jit(solution)/shard_map/pick_rows/pallas_call | solution.py:484
  273.9 4.5 %copy-done.5 = bf16[2,1536,2048]{2,1,0:T(8,128)(2,1)} copy-done((bf16[2,1536,2048]{2,1,0:T(8,128)(2,1)}, bf16[2,1536,2048]{2,1,0:T(8,128)(2,1)S(1)}, u32[]{:S(2)}) %copy-start.5) | copy-done | bytes 12582936
  278.4 16.0 %fusion.44 = f32[2,1536,704]{1,2,0:T(8,128)} fusion(bf16[2,1536,2048]{2,1,0:T(8,128)(2,1)} %copy-done.7, bf16[2,2048,704]{1,2,0:T(8,128)(2,1)} %param.16), kind=kOutput, calls=%fused_computation.79 | convolution fusion | flops 8858370048 | bytes 27000832 | tf_op jit(solution)/shard_map/erd,edf->erf/dot_general | solution.py:542
  294.4 13.3 %fusion.42 = f32[2,1536,704]{1,2,0:T(8,128)} fusion(bf16[2,1536,2048]{2,1,0:T(8,128)(2,1)S(1)} %copy-done.6, bf16[2,704,2048]{2,1,0:T(8,128)(2,1)} %param.18), kind=kOutput, calls=%fused_computation.77 | convolution fusion | flops 8858370048 | bytes 27000832 | tf_op jit(solution)/shard_map/erd,efd->erf/dot_general | solution.py:544
  307.7 11.2 %fusion.1 = f32[2,512,704]{1,2,0:T(8,128)} fusion(f32[2,1536,704]{1,2,0:T(8,128)} %fusion.42, f32[2,1536]{1,0:T(2,128)S(1)} %slice.29, bf16[2,1536,2048]{2,1,0:T(8,128)(2,1)} %copy-done.7, s32[]{:T(128)S(6)} %select_n.61, f32[2,1536,704]{1,2,0:T(8,128)} %fusion.44), kind=kOutput, calls=%fused_computation.6 | convolution fusion | flops 2229731328 | bytes 23343108 | tf_op jit(solution)/shard_map/erm,ern->emn/dot_general | solution.py:678
  318.9 16.5 %fusion.43 = f32[2,1536,704]{1,2,0:T(8,128)} fusion(bf16[2,1536,2048]{2,1,0:T(8,128)(2,1)} %copy-done.7, bf16[2,2048,704]{1,2,0:T(8,128)(2,1)} %param.17), kind=kOutput, calls=%fused_computation.78 | convolution fusion | flops 8858370048 | bytes 27000832 | tf_op jit(solution)/shard_map/erd,edf->erf/dot_general | solution.py:543
  335.4 8.9 %fusion.5 = f32[2,512,704]{1,2,0:T(8,128)S(1)} fusion(f32[2,1536,704]{1,2,0:T(8,128)S(1)} %bitcast.101, f32[2,1536,704]{1,2,0:T(8,128)} %fusion.43, f32[2,1536,704]{1,2,0:T(8,128)} %fusion.42, f32[2,1536]{1,0:T(2,128)S(1)} %slice.29, bf16[2,1536,2048]{2,1,0:T(8,128)(2,1)} %copy-done.7, s32[]{:T(128)S(6)} %select_n.61), kind=kOutput, calls=%fused_computation.10 | convolution fusion | flops 2238382080 | bytes 31993860 | tf_op jit(solution)/shard_map/erm,ern->emn/dot_general | solution.py:678
  344.3 8.9 %attend_back.1 = (bf16[128,2048]{1,0:T(8,128)(2,1)}, bf16[128,2048]{1,0:T(8,128)(2,1)}, bf16[512,1024]{1,0:T(8,128)(2,1)}) custom-call(bf16[128,2048]{1,0:T(8,128)(2,1)} %bitcast.81, bf16[128,2048]{1,0:T(8,128)(2,1)} %bitcast.94, bf16[512,1024]{1,0:T(8,128)(2,1)} %bitcast.97, bf16[128,2048]{1,0:T(8,128)(2,1)} %get-tuple-element.19.att, ...), custom_call_target="tpu_custom_call" | custom-call | flops 1342177280 | bytes 5767168 | tf_op jit(solution)/shard_map/attend_back/pallas_call | solution.py:447
  353.2 11.0 %fusion.2 = f32[2,704,512]{2,1,0:T(8,128)} fusion(f32[2,1536,704]{1,2,0:T(8,128)} %fusion.43, f32[2,1536]{1,0:T(2,128)S(1)} %slice.29, bf16[2,1536,2048]{2,1,0:T(8,128)(2,1)} %copy-done.5, s32[]{:T(128)S(6)} %select_n.61, f32[2,1536,704]{1,2,0:T(8,128)} %fusion.44), kind=kOutput, calls=%fused_computation.7 | convolution fusion | flops 2229731328 | bytes 23343108 | tf_op jit(solution)/shard_map/erm,ern->emn/dot_general | solution.py:678
  364.2 4.5 %add_convert_fusion.2 = bf16[2,512,704]{1,2,0:T(8,128)(2,1)} fusion(f32[2,512,704]{1,2,0:T(8,128)} %fusion.1, bf16[2,512,704]{1,2,0:T(8,128)(2,1)} %copy-done.16, bf16[2,512,2048]{2,1,0:T(8,128)(2,1)S(1)} %copy-done.9, s32[]{:T(128)S(6)} %select_n.61), kind=kOutput, calls=%fused_computation.14 | convolution fusion | flops 739639296 | bytes 6815748 | tf_op jit(solution)/shard_map/erm,ern->emn/dot_general | solution.py:677
  (99 shorter events, 33.5 us)
Async XLA Ops:
  7.2 337.1 %reduce-scatter.6.cloned.1.call-start = ((), (), s32[]{:S(2)}) async-start(), calls=%async_computation.5 | async-start | bytes 4718592 | tf_op jit(solution)/shard_map/reduce_scatter | solution.py:648
  7.9 159.8 %copy-start.20 = (s32[1,128,6]{1,2,0:T(8,128)}, s32[1,128,6]{1,2,0:T(8,128)S(1)}, u32[]{:S(2)}) copy-start(s32[1,128,6]{1,2,0:T(8,128)S(1)} %copy.52) | copy-start | bytes 9220
  169.0 8.6 %copy-start.18 = (f32[2,2048]{1,0:T(2,128)}, f32[2,2048]{1,0:T(2,128)S(1)}, u32[]{:S(2)}) copy-start(f32[2,2048]{1,0:T(2,128)S(1)} %reshape.100) | copy-start | bytes 49156
  169.1 5.8 %copy-start.1 = (bf16[4,2,2,2,128,2048]{5,4,3,2,1,0:T(8,128)(2,1)S(1)}, bf16[4,2,2,2,128,2048]{5,4,3,2,1,0:T(8,128)(2,1)}, u32[]{:S(2)}) copy-start(bf16[4,2,2,2,128,2048]{5,4,3,2,1,0:T(8,128)(2,1)} %get-tuple-element.21) | copy-start | bytes 50331652
  177.7 4.8 %copy-start.8 = (bf16[2,512,2048]{2,1,0:T(8,128)(2,1)}, bf16[2,512,2048]{2,1,0:T(8,128)(2,1)S(1)}, u32[]{:S(2)}) copy-start(bf16[2,512,2048]{2,1,0:T(8,128)(2,1)S(1)} %pick_rows.4) | copy-start | bytes 12582916
  177.7 12.4 %slice-start = ((s8[16777216]{0:T(1024)(128)(4,1)}), s8[4194304]{0:T(1024)(128)(4,1)S(1)}, s32[]{:S(2)}) async-start(s8[16777216]{0:T(1024)(128)(4,1)} %bitcast.67), calls=%async_computation.7 | async-start | bytes 8388608
  177.7 12.4 %slice-start.1 = ((s8[16777216]{0:T(1024)(128)(4,1)}), s8[4194304]{0:T(1024)(128)(4,1)S(1)}, s32[]{:S(2)}) async-start(s8[16777216]{0:T(1024)(128)(4,1)} %bitcast.67), calls=%async_computation.8 | async-start | bytes 8388608
  182.4 7.6 %slice-start.2 = ((s8[16777216]{0:T(1024)(128)(4,1)}), s8[4194304]{0:T(1024)(128)(4,1)S(1)}, s32[]{:S(2)}) async-start(s8[16777216]{0:T(1024)(128)(4,1)} %bitcast.67), calls=%async_computation.9 | async-start | bytes 8388608
  182.4 7.6 %slice-start.3 = ((s8[16777216]{0:T(1024)(128)(4,1)}), s8[4194304]{0:T(1024)(128)(4,1)S(1)}, s32[]{:S(2)}) async-start(s8[16777216]{0:T(1024)(128)(4,1)} %bitcast.67), calls=%async_computation.10 | async-start | bytes 8388608
  192.8 10.0 %copy-start.10 = (bf16[2,512,2048]{2,1,0:T(8,128)(2,1)}, bf16[2,512,2048]{2,1,0:T(8,128)(2,1)S(1)}, u32[]{:S(2)}) copy-start(bf16[2,512,2048]{2,1,0:T(8,128)(2,1)S(1)} %pick_rows.5) | copy-start | bytes 12582916
  202.8 7.3 %copy-start.12 = (bf16[2,512,704]{1,2,0:T(8,128)(2,1)}, bf16[2,512,704]{1,2,0:T(8,128)(2,1)S(1)}, u32[]{:S(2)}) copy-start(bf16[2,512,704]{1,2,0:T(8,128)(2,1)S(1)} %get-tuple-element.50) | copy-start | bytes 4325380
  202.8 7.3 %copy-start.16 = (bf16[2,512,704]{1,2,0:T(8,128)(2,1)}, bf16[2,512,704]{1,2,0:T(8,128)(2,1)S(1)}, u32[]{:S(2)}) copy-start(bf16[2,512,704]{1,2,0:T(8,128)(2,1)S(1)} %get-tuple-element.52) | copy-start | bytes 4325380
  202.8 25.4 %copy-start.14 = (bf16[2,512,704]{1,2,0:T(8,128)(2,1)}, bf16[2,512,704]{1,2,0:T(8,128)(2,1)S(1)}, u32[]{:S(2)}) copy-start(bf16[2,512,704]{1,2,0:T(8,128)(2,1)S(1)} %get-tuple-element.51) | copy-start | bytes 4325380
  224.4 149.6 %all-to-all-start = ((f32[8,2,128]{2,1,0:T(2,128)}), f32[8,2,128]{2,1,0:T(2,128)S(1)}, u32[]{:S(2)}, u32[]{:S(2)}) async-start(f32[8,2,128]{2,1,0:T(2,128)} %select_reduce_fusion.1), calls=%async_computation.3 | async-start | bytes 16384 | tf_op jit(solution)/shard_map/all_to_all | solution.py:663
  228.1 146.5 %reduce-scatter.4.cloned.1.call-start = ((), (), s32[]{:S(2)}) async-start(), calls=%async_computation.4 | async-start | bytes 4718592 | tf_op jit(solution)/shard_map/reduce_scatter | solution.py:654
  235.0 6.2 %copy-start.19 = (f32[2,2048]{1,0:T(2,128)S(1)}, f32[2,2048]{1,0:T(2,128)}, u32[]{:S(2)}) copy-start(f32[2,2048]{1,0:T(2,128)} %copy-done.18) | copy-start | bytes 49156
  241.1 138.8 %reduce-scatter.8.cloned.1.call-start = ((), (), s32[]{:S(2)}) async-start(), calls=%async_computation.6 | async-start | bytes 1310720 | tf_op jit(solution)/shard_map/reduce_scatter | solution.py:689
  241.1 6.5 %copy-start.2 = (bf16[4,2,2,2,128,2048]{5,4,3,2,1,0:T(8,128)(2,1)S(1)}, bf16[4,2,2,2,128,2048]{5,4,3,2,1,0:T(8,128)(2,1)}, u32[]{:S(2)}) copy-start(bf16[4,2,2,2,128,2048]{5,4,3,2,1,0:T(8,128)(2,1)} %get-tuple-element.21) | copy-start | bytes 50331652
  260.1 5.8 %copy-start = (bf16[4,2,2,2,128,2048]{5,4,3,2,1,0:T(8,128)(2,1)S(1)}, bf16[4,2,2,2,128,2048]{5,4,3,2,1,0:T(8,128)(2,1)}, u32[]{:S(2)}) copy-start(bf16[4,2,2,2,128,2048]{5,4,3,2,1,0:T(8,128)(2,1)} %get-tuple-element.25) | copy-start | bytes 50331652
  278.4 16.0 %copy-start.6 = (bf16[2,1536,2048]{2,1,0:T(8,128)(2,1)S(1)}, bf16[2,1536,2048]{2,1,0:T(8,128)(2,1)}, u32[]{:S(2)}) copy-start(bf16[2,1536,2048]{2,1,0:T(8,128)(2,1)} %copy-done.5) | copy-start | bytes 37748740
  307.7 27.7 %slice-start.5 = ((s8[8650752]{0:T(1024)(128)(4,1)}), s8[262144]{0:T(1024)(128)(4,1)S(1)}, s32[]{:S(2)}) async-start(s8[8650752]{0:T(1024)(128)(4,1)} %bitcast.100), calls=%async_computation.12 | async-start | bytes 524288
  307.7 27.7 %slice-start.6 = ((s8[8650752]{0:T(1024)(128)(4,1)}), s8[4194304]{0:T(1024)(128)(4,1)S(1)}, s32[]{:S(2)}) async-start(s8[8650752]{0:T(1024)(128)(4,1)} %bitcast.100), calls=%async_computation.13 | async-start | bytes 8388608
  318.9 16.5 %slice-start.7 = ((s8[8650752]{0:T(1024)(128)(4,1)}), s8[4194304]{0:T(1024)(128)(4,1)S(1)}, s32[]{:S(2)}) async-start(s8[8650752]{0:T(1024)(128)(4,1)} %bitcast.100), calls=%async_computation.14 | async-start | bytes 8388608
  353.2 11.0 %copy-start.9 = (bf16[2,512,2048]{2,1,0:T(8,128)(2,1)S(1)}, bf16[2,512,2048]{2,1,0:T(8,128)(2,1)}, u32[]{:S(2)}) copy-start(bf16[2,512,2048]{2,1,0:T(8,128)(2,1)} %copy-done.8) | copy-start | bytes 12582916
  (11 other events, 35.5 us)
Sparse Core Ops, SparseCore 0:
  223.3 50.8 reduce-scatter.5
  277.5 51.1 reduce-scatter.3
  353.4 26.4 reduce-scatter.7
